TPU v7x, 32 devices: a whole 2x2x4 slice. The times are simulated.
32 devices in a mesh: fsdp: 4 (over z), ctx: 4 (over y, x), tp: 2 (over core).
Axes of the slice: x: 2, y: 2, z: 4, core: 2. Of those that a mesh axis runs over, the one named last changes fastest.
Arguments:
- tokens: bfloat16 [4096, 1024], P(('fsdp', 'ctx')), may hold values from -6 to 6
- lengths: int32 [4, 4], P('fsdp'), may hold values from 1 to 959, as said below
- norm_gain: bfloat16 [1024], P('fsdp'), may hold values from 0.5 to 1.5
- qkv_weight: bfloat16 [3, 1024, 1024], P(None, 'fsdp', 'tp'), may hold values from -0.1875 to 0.1875
- beta_weight: bfloat16 [1024, 8], P('fsdp', 'tp'), may hold values from -0.1875 to 0.1875
- conv_weight: bfloat16 [3, 4, 8, 128], P(None, None, 'tp', 'fsdp'), may hold values from -3 to 3
- head_gain: bfloat16 [128], P('fsdp'), may hold values from 0.5 to 1.5
- out_weight: bfloat16 [1024, 1024], P('tp', 'fsdp'), may hold values from -0.1875 to 0.1875
- mlp_gain: bfloat16 [1024], P('fsdp'), may hold values from 0.5 to 1.5
- gate_up_weight: bfloat16 [2, 1024, 2816], P(None, 'fsdp', 'tp'), may hold values from -0.1875 to 0.1875
- down_weight: bfloat16 [2816, 1024], P('tp', 'fsdp'), may hold values from -0.15625 to 0.15625
- cotangent: bfloat16 [4096, 1024], P(('fsdp', 'ctx')), may hold values from -6 to 6
Outputs:
- layer_out: bfloat16 [4096, 1024], P(('fsdp', 'ctx'))
- input_grad: float32 [4096, 1024], P(('fsdp', 'ctx'))
- norm_gain_grad: float32 [1024], P('fsdp')
- qkv_grad: float32 [3, 1024, 1024], P(None, 'fsdp', 'tp')
- beta_grad: float32 [1024, 8], P('fsdp', 'tp')
- conv_grad: float32 [3, 4, 8, 128], P(None, None, 'tp', 'fsdp')
- head_gain_grad: float32 [128], P('fsdp')
- out_grad: float32 [1024, 1024], P('tp', 'fsdp')
- mlp_gain_grad: float32 [1024], P('fsdp')
- gate_up_grad: float32 [2, 1024, 2816], P(None, 'fsdp', 'tp')
- down_grad: float32 [2816, 1024], P('tp', 'fsdp')
- rms: float32 [5], replicated
Inputs may be any that keep to these rules, and one draw needn't show every extreme that they name: Row g lists the 4 sequence lengths of stream g in order; they sum to at most 1024, the remaining slots at the end are padding. The second sequence of each stream ends at slot 960, so it includes a slot of the first and of the last of its 4 blocks of 256 slots.
All inputs are finite; a program needn't handle non-finite values.
Results may differ from a plain program's by a relative error of at most 0.012.
The roundings to bfloat16 on the way count: a program that leaves them out, or rounds other values in their place, can miss the bound.
Values may be sent and summed in bfloat16 or wider, within the bound.
No kernel may reach another device: no remote copies, remote signals or barrier semaphores. Data moves between devices by JAX's collectives and lax.ppermute only.
A program may use at most 128 MiB of HBM per device.

v0:
```python
import jax
import jax.numpy as jnp
from jax import lax
from jax.sharding import PartitionSpec as P

D = 1024
HD = 128
C = 64
CONV = 4
PRECISE = lax.Precision.HIGHEST
NORM_EPS = 1e-06


def passed_along(value, axis, steps):
    count = lax.axis_size(axis)
    leading, last = (max(0, -steps), min(count, count - steps))
    return lax.ppermute(value, axis, [(source, source + steps) for source in range(leading, last)])


def product(form, left, right):
    return jnp.einsum(form, left, right, precision=PRECISE)


def rounded(values):
    return lax.optimization_barrier(values.astype(jnp.bfloat16)).astype(jnp.float32)


def rms_norm(values, gain):
    return values * lax.rsqrt(jnp.mean(values * values, -1, keepdims=True) + NORM_EPS) * gain


def norm_back(values, gain, grad):
    ratio = lax.rsqrt(jnp.mean(values * values, -1, keepdims=True) + NORM_EPS)
    scaled = values * ratio
    weighted = grad * gain
    value_grad = ratio * (weighted - scaled * jnp.mean(weighted * scaled, -1, keepdims=True))
    gain_grad = jnp.sum((grad * scaled).reshape(-1, values.shape[-1]), 0)
    return (value_grad, gain_grad)


def l2_norm(values):
    return values * lax.rsqrt(jnp.sum(values * values, -1, keepdims=True) + NORM_EPS)


def seq_layout(lengths_row, first, row_count):
    ends = jnp.cumsum(lengths_row)
    places = first + jnp.arange(row_count, dtype=jnp.int32)
    passed = ends[None, :] <= places[:, None]
    begins = jnp.max(jnp.where(passed, ends[None, :], 0), -1)
    seg_ids = jnp.sum(passed.astype(jnp.int32), -1)
    valid = (places < ends[-1]).astype(jnp.float32)
    resets = places == begins
    offsets = places[:, None] - (CONV - 1) + jnp.arange(CONV, dtype=jnp.int32)[None, :]
    taps = (offsets >= begins[:, None]).astype(jnp.float32)
    return (seg_ids, resets, valid, taps)


def block_masks(seg_ids, resets):
    seg_blocks = seg_ids.reshape(-1, C)
    same_seq = (seg_blocks[:, :, None] == seg_blocks[:, None, :]).astype(jnp.float32)
    reset_count = jnp.cumsum(resets.reshape(-1, C).astype(jnp.int32), -1)
    carried = (reset_count == 0).astype(jnp.float32)
    return (same_seq, carried)


def conv_heads(extended, conv_taps, taps):
    row_count = taps.shape[0]
    total = jnp.zeros((row_count,) + extended.shape[1:], jnp.float32)
    for offset in range(CONV):
        total = (
            total
            + extended[offset : offset + row_count]
            * conv_taps[:, offset][None]
            * taps[:, offset][:, None, None]
        )
    activated = jax.nn.silu(total)
    head_count = extended.shape[2] // HD
    split_rows = activated.reshape(row_count, 3, head_count, HD)
    return (l2_norm(split_rows[:, 0]), l2_norm(split_rows[:, 1]), split_rows[:, 2])


def to_blocks(values):
    return values.reshape(values.shape[0] // C, C, values.shape[1], values.shape[2]).transpose(
        2, 0, 1, 3
    )


def beta_blocks(values):
    return values.reshape(values.shape[0] // C, C, values.shape[1]).transpose(2, 0, 1)


def from_blocks(values):
    return values.transpose(1, 2, 0, 3).reshape(-1, values.shape[0], values.shape[3])


def unit_inverse(lower):
    size_now = lower.shape[-1]
    identity = jnp.eye(size_now, dtype=jnp.float32)
    inverse = identity - lower
    power = lower
    span = 2
    while span < size_now:
        power = product("...ij,...jk->...ik", power, power)
        inverse = product("...ij,...jk->...ik", inverse, identity + power)
        span = span * 2
    return inverse


def block_terms(queries, key_rows, value_rows, beta_rows, same_seq, carried):
    wide = key_rows.shape[-1]
    last_seg = same_seq[:, -1, :]
    key_gram = product("hncd,hnmd->hncm", key_rows, key_rows)
    lower = jnp.tril(beta_rows[..., :, None] * key_gram * same_seq, -1)
    inverse = unit_inverse(lower)
    stacked = beta_rows[..., None] * jnp.concatenate([key_rows, value_rows], -1)
    solved = product("hncm,hnmd->hncd", inverse, stacked)
    w_part = solved[..., :wide]
    u_part = solved[..., wide:]
    query_key = jnp.tril(product("hncd,hnmd->hncm", queries, key_rows) * same_seq)
    keep_all = carried[:, -1]
    trans = keep_all[:, None, None] * jnp.eye(wide, dtype=jnp.float32) - product(
        "hnci,hncj->hnij", w_part * (carried * last_seg)[..., None], key_rows
    )
    push = product("hnci,hncj->hnij", u_part * last_seg[..., None], key_rows)
    return (w_part, u_part, query_key, queries, trans, push)


def run_blocks(terms, carried, start_state):
    sequenced = tuple((jnp.moveaxis(piece, 1, 0) for piece in terms)) + (carried,)

    def advance(state, pieces):
        w_now, u_now, qk_now, q_now, trans_now, push_now, carry_now = pieces
        carry_col = carry_now[None, :, None]
        from_state = product("hcd,hvd->hcv", w_now, state)
        fresh = u_now - carry_col * from_state
        output = carry_col * product("hcd,hvd->hcv", q_now, state) + product(
            "hcm,hmv->hcv", qk_now, fresh
        )
        following = product("hvk,hkj->hvj", state, trans_now) + push_now
        return (following, output)

    final_state, outputs = lax.scan(advance, start_state, sequenced)
    return (jnp.moveaxis(outputs, 0, 1), final_state)


def join_maps(earlier, later):
    return (
        product("hik,hkj->hij", earlier[0], later[0]),
        product("hvk,hkj->hvj", earlier[1], later[0]) + later[1],
    )


def row_total(values, valid):
    return jnp.sum(valid * jnp.sum(values * values, -1))


def local(
    tokens,
    lengths,
    norm_gain,
    qkv_weight,
    beta_weight,
    conv_weight,
    head_gain,
    out_weight,
    mlp_gain,
    gate_up_weight,
    down_weight,
    cotangent,
):
    row_count = tokens.shape[0]
    ctx_count = lax.axis_size("ctx")
    fsdp_count = lax.axis_size("fsdp")
    seg_ids, resets, valid, taps = seq_layout(
        lengths[0], lax.axis_index("ctx") * row_count, row_count
    )
    same_seq, carried = block_masks(seg_ids, resets)
    gathered = (
        lax.all_gather(norm_gain, "fsdp", axis=0, tiled=True),
        lax.all_gather(qkv_weight, "fsdp", axis=1, tiled=True),
        lax.all_gather(beta_weight, "fsdp", axis=0, tiled=True),
        lax.all_gather(conv_weight, "fsdp", axis=3, tiled=True),
        lax.all_gather(head_gain, "fsdp", axis=0, tiled=True),
        lax.all_gather(out_weight, "fsdp", axis=1, tiled=True),
        lax.all_gather(mlp_gain, "fsdp", axis=0, tiled=True),
        lax.all_gather(gate_up_weight, "fsdp", axis=1, tiled=True),
        lax.all_gather(down_weight, "fsdp", axis=1, tiled=True),
    )
    (
        first_gain,
        qkv_full,
        beta_full,
        conv_full,
        head_full,
        out_full,
        second_gain,
        gate_up_full,
        down_full,
    ) = gathered
    heads_local = beta_full.shape[1]
    width_local = qkv_full.shape[2]
    x_wide = tokens.astype(jnp.float32)
    first_f = first_gain.astype(jnp.float32)
    second_f = second_gain.astype(jnp.float32)
    head_f = head_full.astype(jnp.float32)
    normed_in = rms_norm(x_wide, first_f).astype(jnp.bfloat16)
    projected = jnp.einsum(
        "td,idk->tik", normed_in, qkv_full, preferred_element_type=jnp.float32
    ).astype(jnp.bfloat16)
    beta_rows = jax.nn.sigmoid(jnp.dot(normed_in, beta_full, preferred_element_type=jnp.float32))
    rim_rows = passed_along(projected[row_count - (CONV - 1) :], "ctx", 1)
    extended = jnp.concatenate([rim_rows, projected], 0).astype(jnp.float32)
    conv_local = conv_full.reshape(3, CONV, width_local).astype(jnp.float32)

    def conv_part(ext_rows, conv_taps):
        return conv_heads(ext_rows, conv_taps, taps)

    (query_raw, key_raw, value_raw), conv_pull = jax.vjp(conv_part, extended, conv_local)
    queries = rounded(query_raw)
    key_rows = rounded(key_raw)
    value_rows = rounded(value_raw)

    def prepare(query_in, key_in, value_in, beta_in):
        return block_terms(
            to_blocks(query_in) * HD ** (-0.5),
            to_blocks(key_in),
            to_blocks(value_in),
            beta_blocks(beta_in),
            same_seq,
            carried,
        )

    terms, prepare_pull = jax.vjp(prepare, queries, key_rows, value_rows, beta_rows)
    identity = jnp.broadcast_to(jnp.eye(HD, dtype=jnp.float32), (heads_local, HD, HD))
    empty_state = jnp.zeros((heads_local, HD, HD), jnp.float32)

    def compose(accum, pieces):
        return (join_maps(accum, pieces), None)

    (device_map, device_shift), ignored = lax.scan(
        compose,
        (identity, empty_state),
        (jnp.moveaxis(terms[4], 1, 0), jnp.moveaxis(terms[5], 1, 0)),
    )
    incoming = empty_state
    for repeat in range(ctx_count - 1):
        incoming = passed_along(
            product("hvk,hkj->hvj", incoming, device_map) + device_shift, "ctx", 1
        )

    def run_part(term_in, state_in):
        return run_blocks(term_in, carried, state_in)

    (out_blocks, ignored_state), run_pull = jax.vjp(run_part, terms, incoming)
    mixed_out = from_blocks(out_blocks)
    head_normed = rms_norm(mixed_out, head_f).reshape(row_count, width_local).astype(jnp.bfloat16)
    attn_rows = (
        lax.psum(jnp.dot(head_normed, out_full, preferred_element_type=jnp.float32), "tp")
        * valid[:, None]
    )
    middle = x_wide + attn_rows
    normed_mid = rms_norm(middle, second_f).astype(jnp.bfloat16)
    gate_up = jnp.einsum(
        "td,idf->tif", normed_mid, gate_up_full, preferred_element_type=jnp.float32
    )
    gate_rows = gate_up[:, 0]
    up_rows = gate_up[:, 1]
    activated = (jax.nn.silu(gate_rows) * up_rows).astype(jnp.bfloat16)
    ffn_rows = (
        lax.psum(jnp.dot(activated, down_full, preferred_element_type=jnp.float32), "tp")
        * valid[:, None]
    )
    result = middle + ffn_rows
    stat_sums = jnp.stack(
        [
            row_total(x_wide, valid),
            row_total(attn_rows, valid),
            row_total(middle, valid),
            row_total(ffn_rows, valid),
            row_total(result, valid),
            jnp.sum(valid),
        ]
    )
    out_cot = cotangent.astype(jnp.float32)
    ffn_back = (out_cot * valid[:, None]).astype(jnp.bfloat16)
    down_grad = jnp.einsum("tf,td->fd", activated, ffn_back, preferred_element_type=jnp.float32)
    act_grad = jnp.einsum("td,fd->tf", ffn_back, down_full, preferred_element_type=jnp.float32)
    gate_sig = jax.nn.sigmoid(gate_rows)
    up_grad = act_grad * gate_rows * gate_sig
    gate_grad = act_grad * up_rows * gate_sig * (1.0 + gate_rows * (1.0 - gate_sig))
    gate_up_back = jnp.stack([gate_grad, up_grad], 1).astype(jnp.bfloat16)
    gate_up_grad = jnp.einsum(
        "td,tif->idf", normed_mid, gate_up_back, preferred_element_type=jnp.float32
    )
    mid_part = jnp.einsum(
        "tif,idf->td", gate_up_back, gate_up_full, preferred_element_type=jnp.float32
    )
    mid_grad = lax.psum(mid_part, "tp")
    middle_norm_grad, second_gain_grad = norm_back(middle, second_f, mid_grad)
    middle_grad = out_cot + middle_norm_grad
    attn_back = (middle_grad * valid[:, None]).astype(jnp.bfloat16)
    out_grad = jnp.einsum("tk,td->kd", head_normed, attn_back, preferred_element_type=jnp.float32)
    head_in_grad = jnp.einsum(
        "td,kd->tk", attn_back, out_full, preferred_element_type=jnp.float32
    ).reshape(row_count, heads_local, HD)
    mixed_grad, head_gain_part = norm_back(mixed_out, head_f, head_in_grad)
    mixed_blocks = to_blocks(mixed_grad)

    def state_part(state_in):
        return run_blocks(terms, carried, state_in)[0]

    ignored_out, state_pull = jax.vjp(state_part, incoming)
    local_state = state_pull(mixed_blocks)[0]
    map_turned = jnp.swapaxes(device_map, 1, 2)
    outgoing = empty_state
    for repeat in range(ctx_count - 1):
        outgoing = passed_along(
            local_state + product("hvk,hkj->hvj", outgoing, map_turned), "ctx", -1
        )
    term_grads, ignored_grad = run_pull((mixed_blocks, outgoing))
    query_grad, key_grad, value_grad, beta_row_grad = prepare_pull(term_grads)
    logit_grad = (beta_row_grad * beta_rows * (1.0 - beta_rows)).astype(jnp.bfloat16)
    ext_grad, conv_grad_flat = conv_pull((query_grad, key_grad, value_grad))
    back_rim = passed_along(ext_grad[: CONV - 1], "ctx", -1)
    proj_grad = ext_grad[CONV - 1 :] + jnp.concatenate(
        [jnp.zeros((row_count - (CONV - 1),) + back_rim.shape[1:], jnp.float32), back_rim], 0
    )
    proj_back = proj_grad.astype(jnp.bfloat16)
    qkv_grad = jnp.einsum("td,tik->idk", normed_in, proj_back, preferred_element_type=jnp.float32)
    beta_grad = jnp.einsum("td,th->dh", normed_in, logit_grad, preferred_element_type=jnp.float32)
    in_part = jnp.einsum(
        "tik,idk->td", proj_back, qkv_full, preferred_element_type=jnp.float32
    ) + jnp.einsum("th,dh->td", logit_grad, beta_full, preferred_element_type=jnp.float32)
    in_grad, head_gain_grad = lax.psum((in_part, head_gain_part), "tp")
    x_norm_grad, first_gain_grad = norm_back(x_wide, first_f, in_grad)
    input_grad = middle_grad + x_norm_grad
    stat_rows = jnp.broadcast_to(stat_sums[None, :], (fsdp_count, stat_sums.shape[0]))
    conv_grad = conv_grad_flat.reshape(3, CONV, heads_local, HD)
    shares = (
        lax.psum_scatter(first_gain_grad, "fsdp", scatter_dimension=0, tiled=True),
        lax.psum_scatter(qkv_grad, "fsdp", scatter_dimension=1, tiled=True),
        lax.psum_scatter(beta_grad, "fsdp", scatter_dimension=0, tiled=True),
        lax.psum_scatter(conv_grad, "fsdp", scatter_dimension=3, tiled=True),
        lax.psum_scatter(head_gain_grad, "fsdp", scatter_dimension=0, tiled=True),
        lax.psum_scatter(out_grad, "fsdp", scatter_dimension=1, tiled=True),
        lax.psum_scatter(second_gain_grad, "fsdp", scatter_dimension=0, tiled=True),
        lax.psum_scatter(gate_up_grad, "fsdp", scatter_dimension=1, tiled=True),
        lax.psum_scatter(down_grad, "fsdp", scatter_dimension=1, tiled=True),
        lax.psum_scatter(stat_rows, "fsdp", scatter_dimension=0, tiled=True),
    )
    totals = lax.psum(
        (
            shares[0],
            shares[1],
            shares[2],
            shares[3],
            shares[4],
            shares[5],
            shares[6],
            shares[7],
            shares[8],
            shares[9],
        ),
        "ctx",
    )
    stat_total = totals[9][0]
    rms = jnp.sqrt(stat_total[:5] / (stat_total[5] * D))
    return (
        result.astype(jnp.bfloat16),
        input_grad,
        totals[0],
        totals[1],
        totals[2],
        totals[3],
        totals[4],
        totals[5],
        totals[6],
        totals[7],
        totals[8],
        rms,
    )


def solution(mesh):
    return jax.shard_map(
        local,
        mesh=mesh,
        in_specs=(
            P(("fsdp", "ctx"), None),
            P("fsdp", None),
            P("fsdp"),
            P(None, "fsdp", "tp"),
            P("fsdp", "tp"),
            P(None, None, "tp", "fsdp"),
            P("fsdp"),
            P("tp", "fsdp"),
            P("fsdp"),
            P(None, "fsdp", "tp"),
            P("tp", "fsdp"),
            P(("fsdp", "ctx"), None),
        ),
        out_specs=(
            P(("fsdp", "ctx"), None),
            P(("fsdp", "ctx"), None),
            P("fsdp"),
            P(None, "fsdp", "tp"),
            P("fsdp", "tp"),
            P(None, None, "tp", "fsdp"),
            P("fsdp"),
            P("tp", "fsdp"),
            P("fsdp"),
            P(None, "fsdp", "tp"),
            P("tp", "fsdp"),
            P(),
        ),
        check_vma=False,
    )
```

profile of v0, /device:TPU:0, one launch (start us, length us, event | category | flops | bytes accessed | tf_op | source)
XLA Modules:
  0.0 1154.2 jit_solution(13363397626016956386)
XLA Ops:
  10.7 12.6 %all-gather = bf16[4,1,256]{2,1,0:T(2,128)(2,1)S(1)} all-gather(bf16[1,1,256]{2,1,0:T(2,128)(2,1)S(1)} %reshape.331), channel_id=1, replica_groups=mesh['fsdp'=4,'ctx'=4,'tp'=2] {'fsdp'}, dimensions={0}, use_global_device_ids=true | all-gather | bytes 2560 | tf_op jit(solution)/shard_map/all_gather | solution.py:179
  24.0 17.8 %all_gather.30 = bf16[3,4,4,128]{2,1,0,3:T(4,128)(2,1)S(1)} all-gather(bf16[3,4,4,32]{2,1,0,3:T(4,128)(2,1)S(1)} %copy.589), channel_id=1, replica_groups=mesh['fsdp'=4,'ctx'=4,'tp'=2] {'fsdp'}, dimensions={3}, use_global_device_ids=true | all-gather | bytes 15360 | tf_op jit(solution)/shard_map/all_gather | solution.py:182
  42.4 12.2 %all_gather.28 = bf16[1024,4]{0,1:T(4,128)(2,1)S(1)} all-gather(bf16[256,4]{0,1:T(4,128)(2,1)S(1)} %copy-done.132), channel_id=1, replica_groups=mesh['fsdp'=4,'ctx'=4,'tp'=2] {'fsdp'}, dimensions={0}, use_global_device_ids=true | all-gather | bytes 10240 | tf_op jit(solution)/shard_map/all_gather | solution.py:181
  57.8 11.3 all-reduce.14
  70.2 11.6 %all-gather.7.cloned.1.call-done = bf16[3,1024,512]{2,1,0:T(8,128)(2,1)} async-done(((bf16[3,256,512]{2,1,0:T(8,128)(2,1)}), bf16[3,1024,512]{2,1,0:T(8,128)(2,1)}) %all-gather.7.cloned.1.call-update) | async-done | bytes 3145744 | tf_op jit(solution)/shard_map/all_gather | solution.py:180
  81.8 2.9 convolution_convert_fusion
  84.8 3.4 collective-permute-start
  89.8 2.9 fusion.96
  92.7 2.9 reshape.310
  121.0 2.5 copy.609
  127.2 13.8 %while.85 = (s32[]{:T(128)}, f32[4,128,128]{1,2,0:T(8,128)S(1)}, f32[4,128,128]{1,2,0:T(8,128)}, f32[4,4,128,128]{2,3,1,0:T(8,128)S(1)}, f32[4,4,128,128]{2,3,1,0:T(8,128)}, /*index=5*/s32[]{:T(128)}, s32[]{:T(128)}) while((s32[]{:T(128)}, f32[4,128,128]{1,2,0:T(8,128)S(1)}, f32[4,128,128]{1,2,0:T(8,128)}, ...), condition=%wide.region_7.8_spmd.clone, body=%wide.region_6.7_spmd.clone.sunk | while | flops 201457664 | bytes 2884699 | solution.py:240
  144.7 4.2 collective-permute-start.1
  150.2 3.1 collective-permute-done.1
  154.0 4.4 collective-permute-start.2
  159.3 2.9 collective-permute-done.2
  162.9 5.9 collective-permute-start.3
  173.9 33.4 %while.82 = (s32[]{:T(128)}, f32[4,128,128]{1,2,0:T(8,128)}, f32[4,4,64,128]{3,2,1,0:T(8,128)}, f32[4,4,128,128]{2,3,1,0:T(8,128)S(1)}, f32[4,1,64,1]{2,3,1,0:T(...) while((s32[]{:T(128)}, f32[4,128,128]{1,2,0:T(8,128)}, ...), condition=%wide.region_10.11_spmd, body=%wide.region_9.10_spmd.sunk | while | flops 226689024 | bytes 3937937 | solution.py:142
  212.4 2.7 fusion.248
  216.9 9.6 all-gather.1
  227.7 9.6 all-reduce.28.cloned.1.call-done
  239.1 107.7 %all-gather.11.cloned.1.call-done = bf16[2,1024,1408]{2,1,0:T(8,128)(2,1)} async-done(((bf16[2,256,1408]{2,1,0:T(8,128)(2,1)}), bf16[2,1024,1408]{2,1,0:T(8,128)(2,1)}) %all-gather.11.cloned.1.call-update) | async-done | bytes 5767184 | tf_op jit(solution)/shard_map/all_gather | solution.py:186
  346.8 5.9 fusion.207
  352.7 53.0 %all-gather.13.cloned.1.call-done = bf16[1408,1024]{1,0:T(8,128)(2,1)} async-done(((bf16[1408,256]{1,0:T(8,128)(2,1)}), bf16[1408,1024]{1,0:T(8,128)(2,1)}) %all-gather.13.cloned.1.call-update) | async-done | bytes 2883600 | tf_op jit(solution)/shard_map/all_gather | solution.py:187
  405.7 4.4 fusion.133
  412.2 2.7 convolution_bitcast_fusion.13
  414.9 2.8 while.83
  421.6 12.9 %all-reduce.34.cloned.1.call-done = (f32[256,1024]{1,0:T(8,128)}, f32[256,1024]{1,0:T(8,128)}) async-done(((f32[256,1024]{1,0:T(8,128)}, f32[256,1024]{1,0:T(8,128)}), (f32[256,1024]{1,0:T(8,128)}, f32[256,1024]{1,0:T(8,128)})) %all-reduce.34.cloned.1.call-update) | async-done | bytes 2097168 | tf_op jit(solution)/shard_map/psum | solution.py:270
  434.5 3.9 multiply_reduce_fusion.4
  448.6 22.0 %while.86 = (s32[]{:T(128)}, f32[4,128,128]{1,2,0:T(8,128)}, f32[4,4,128,128]{3,2,1,0:T(8,128)}, f32[4,1,64,1]{2,3,1,0:T(1,128)S(1)}, f32[4,4,64,128]{3,2,1,0:T(...) while((s32[]{:T(128)}, f32[4,128,128]{1,2,0:T(8,128)}, ...), condition=%wide.region_21.22_spmd.clone, body=%wide.region_20.21_spmd.clone.sunk | while | flops 226787328 | bytes 2756239 | solution.py:142
  475.1 9.1 collective-permute-done.4
  486.8 9.3 collective-permute-done.5
  498.5 3.5 fusion.195
  502.1 5.2 collective-permute-done.6
  513.9 51.4 %while.84 = (s32[]{:T(128)}, f32[4,128,128]{1,2,0:T(8,128)S(1)}, f32[4,4,64,128]{3,2,0,1:T(8,128)}, f32[4,4,64,128]{3,2,0,1:T(8,128)}, f32[4,4,64,64]{2,3,1,0:T(...) while((s32[]{:T(128)}, f32[4,128,128]{1,2,0:T(8,128)S(1)}, ...), condition=%wide.region_23.24_spmd, body=%wide.region_22.23_spmd.sunk | while | flops 453312512 | bytes 9840861 | solution.py:142
  606.9 4.2 collective-permute-done.7
  611.2 3.7 convolution_bitcast_fusion.10
  616.1 8.1 convolution_bitcast_fusion.9
  629.4 4.2 fusion.102
  633.7 93.4 %reduce-scatter.11.cloned.1.call-done = f32[3,256,512]{1,2,0:T(8,128)} async-done(((f32[3,1024,512]{1,2,0:T(8,128)}), f32[3,256,512]{1,2,0:T(8,128)}) %reduce-scatter.11.cloned.1.call-update) | async-done | bytes 1572880 | tf_op jit(solution)/shard_map/reduce_scatter | solution.py:341
  727.1 197.8 %reduce-scatter.15.cloned.1.call-done = f32[2,256,1408]{1,2,0:T(8,128)} async-done(((f32[2,1024,1408]{1,2,0:T(8,128)}), f32[2,256,1408]{1,2,0:T(8,128)}) %reduce-scatter.15.cloned.1.call-update) | async-done | bytes 2883600 | tf_op jit(solution)/shard_map/reduce_scatter | solution.py:347
  927.2 4.0 stack.42
  931.4 19.1 %reduce-scatter.19.cloned.1.call-done = f32[256,4]{1,0:T(8,128)} async-done(((f32[1024,4]{1,0:T(8,128)}), f32[256,4]{1,0:T(8,128)}) %reduce-scatter.19.cloned.1.call-update) | async-done | bytes 4112
  951.5 19.1 %reduce-scatter.21.cloned.1.call-done = f32[32,48]{1,0:T(8,128)} async-done(((f32[128,48]{1,0:T(8,128)}), f32[32,48]{1,0:T(8,128)}) %reduce-scatter.21.cloned.1.call-update) | async-done | bytes 6160
  971.6 19.7 %all-reduce.30.cloned.1.call-done = f32[256,1024]{1,0:T(8,128)} async-done(((f32[256,1024]{1,0:T(8,128)}), f32[256,1024]{1,0:T(8,128)}) %all-reduce.30.cloned.1.call-update) | async-done | bytes 1048592 | tf_op jit(solution)/shard_map/psum | solution.py:334
  993.1 19.0 %all-reduce.21 = (f32[1024]{0:T(1024)S(1)}, f32[128]{0:T(128)S(1)}, f32[1024]{0:T(1024)S(1)}, f32[4,6]{1,0:T(4,128)S(1)}) all-reduce(f32[1024]{0:T(1024)S(1)} %get-tuple-element.993, f32[128]{0:T(128)S(1)} %multiply_reduce_fusion.10, f32[1024]{0:T(1024)S(1)} %copy-done.116, ...), channel_id=2, replica_groups=mesh['fsdp'=4,'ctx'=4,'tp'=2] {'fsdp'}, use_global_device_ids=true, to_apply=%region_31.32.clone | all-reduce | flops 2200 | bytes 17600
  1015.3 17.8 %all-reduce.19 = (f32[256]{0:T(256)}, f32[256,4]{0,1:T(4,128)}, f32[3,4,4,32]{3,2,1,0:T(4,128)}, f32[32]{0:T(128)}, f32[256]{0:T(256)}, /*index=5*/f32[1,6]{1,0:T(1,128)S(1)}) all-reduce(f32[256]{0:T(256)S(1)} %dynamic-slice.2, f32[256,4]{0,1:T(4,128)S(1)} %copy.747, ...), channel_id=1, replica_groups=mesh['fsdp'=4,'ctx'=4,'tp'=2] {'ctx'}, use_global_device_ids=true, to_apply=%region_32.33 | all-reduce | flops 3110 | bytes 24880 | tf_op jit(solution)/shard_map/psum | solution.py:351
  1036.2 103.1 %all-reduce.32.cloned.1.call-done = (f32[3,256,512]{1,2,0:T(8,128)}, f32[512,256]{1,0:T(8,128)}, f32[2,256,1408]{1,2,0:T(8,128)}, f32[1408,256]{1,0:T(8,128)}) async-done(((f32[3,256,512]{1,2,0:T(8,128)}, f32[512,256]{1,0:T(8,128)}, f32[2,256,1408]{1,2,0:T(8,128)}, f32[1408,256]{1,0:T(8,128)}), (f32[3,256,512]{1,2,0:T(8,128)}, f32[512,256]{1,0:T(8,128)}, f32[2,256,1408]{1,2,0:T(8,128)}, ...) | async-done | bytes 6422544 | tf_op jit(solution)/shard_map/psum | solution.py:351
  1139.3 3.5 copy.687
  (646 shorter events, 277.6 us)
Async XLA Ops:
  7.2 49.1 %copy-start.134 = (u32[32]{0:T(128)S(1)}, u32[32]{0:T(128)}, u32[]{:S(2)}) copy-start(u32[32]{0:T(128)} %constant.232) | copy-start | bytes 388
  7.2 16.1 %copy-start.140 = (s32[1,4]{1,0:T(1,128)S(1)}, s32[1,4]{1,0:T(1,128)}, u32[]{:S(2)}) copy-start(s32[1,4]{1,0:T(1,128)} %param.23) | copy-start | bytes 52
  7.2 16.5 %copy-start.119 = (bf16[3,4,4,32]{3,2,1,0:T(4,128)(2,1)S(1)}, bf16[3,4,4,32]{3,2,1,0:T(4,128)(2,1)}, u32[]{:S(2)}) copy-start(bf16[3,4,4,32]{3,2,1,0:T(4,128)(2,1)} %param.27) | copy-start | bytes 9220
  7.2 35.2 %copy-start.132 = (bf16[256,4]{0,1:T(4,128)(2,1)S(1)}, bf16[256,4]{0,1:T(4,128)(2,1)}, u32[]{:S(2)}) copy-start(bf16[256,4]{0,1:T(4,128)(2,1)} %param.26) | copy-start | bytes 6148
  7.2 50.3 %copy-start.141 = (bf16[32]{0:T(256)(128)(2,1)S(1)}, bf16[32]{0:T(256)(128)(2,1)}, u32[]{:S(2)}) copy-start(bf16[32]{0:T(256)(128)(2,1)} %param.28) | copy-start | bytes 196
  7.2 62.6 %copy-start.11 = (bf16[256,1024]{1,0:T(8,128)(2,1)S(1)}, bf16[256,1024]{1,0:T(8,128)(2,1)}, u32[]{:S(2)}) copy-start(bf16[256,1024]{1,0:T(8,128)(2,1)} %param.22) | copy-start | bytes 1572868
  7.3 74.5 %all-gather.7.cloned.1.call-start = ((), (), s32[]{:S(2)}) async-start(), calls=%async_computation.6 | async-start | bytes 3932160 | tf_op jit(solution)/shard_map/all_gather | solution.py:180
  8.0 204.4 %all-gather.9.cloned.1.call-start = ((), (), s32[]{:S(2)}) async-start(), calls=%async_computation.7 | async-start | bytes 1310720 | tf_op jit(solution)/shard_map/all_gather | solution.py:184
  8.7 228.6 %all-reduce.28.cloned.1.call-start = ((), (), s32[]{:S(2)}) async-start(), calls=%async_computation.8 | async-start | bytes 2097152 | tf_op jit(solution)/shard_map/psum | solution.py:258
  8.8 61.3 %copy-start.82 = (f32[128,128]{0,1:T(8,128)}, f32[128,128]{0,1:T(8,128)S(1)}, u32[]{:S(2)}) copy-start(f32[128,128]{0,1:T(8,128)S(1)} %fusion.204) | copy-start | bytes 196612
  10.7 74.1 %copy-start.106 = (f32[256]{0:T(256)}, f32[256]{0:T(256)S(1)}, u32[]{:S(2)}) copy-start(f32[256]{0:T(256)S(1)} %add_rsqrt_fusion.4) | copy-start | bytes 3076
  23.7 66.1 %copy-start.108 = (f32[256,1]{0,1:T(1,128)}, f32[256,1]{0,1:T(1,128)S(1)}, u32[]{:S(2)}) copy-start(f32[256,1]{0,1:T(1,128)S(1)} %get-tuple-element.1145) | copy-start | bytes 3076
  23.7 66.1 %copy-start.110 = (f32[256,1]{0,1:T(1,128)}, f32[256,1]{0,1:T(1,128)S(1)}, u32[]{:S(2)}) copy-start(f32[256,1]{0,1:T(1,128)S(1)} %get-tuple-element.1146) | copy-start | bytes 3076
  23.7 66.1 %copy-start.112 = (f32[256,1]{0,1:T(1,128)}, f32[256,1]{0,1:T(1,128)S(1)}, u32[]{:S(2)}) copy-start(f32[256,1]{0,1:T(1,128)S(1)} %get-tuple-element.1147) | copy-start | bytes 3076
  23.7 66.1 %copy-start.114 = (f32[256,1]{0,1:T(1,128)}, f32[256,1]{0,1:T(1,128)S(1)}, u32[]{:S(2)}) copy-start(f32[256,1]{0,1:T(1,128)S(1)} %get-tuple-element.1148) | copy-start | bytes 3076
  54.6 30.1 %copy-start.100 = (bf16[1024,4]{0,1:T(4,128)(2,1)}, bf16[1024,4]{0,1:T(4,128)(2,1)S(1)}, u32[]{:S(2)}) copy-start(bf16[1024,4]{0,1:T(4,128)(2,1)S(1)} %all_gather.28) | copy-start | bytes 24580
  69.7 20.1 %copy-start.84 = (f32[3,512]{1,0:T(4,128)}, f32[3,512]{1,0:T(4,128)S(1)}, u32[]{:S(2)}) copy-start(f32[3,512]{1,0:T(4,128)S(1)} %get-tuple-element.1158) | copy-start | bytes 18436
  70.2 18.1 %copy-start.117 = (f32[256,4]{0,1:T(4,128)}, f32[256,4]{0,1:T(4,128)S(1)}, u32[]{:S(2)}) copy-start(f32[256,4]{0,1:T(4,128)S(1)} %fusion.116) | copy-start | bytes 12292
  84.8 4.8 collective-permute-start
  107.5 41.4 %copy-start.94 = (f32[256,4]{0,1:T(4,128)}, f32[256,4]{0,1:T(4,128)S(1)}, u32[]{:S(2)}) copy-start(f32[256,4]{0,1:T(4,128)S(1)} %fusion.147) | copy-start | bytes 12292
  144.7 8.6 collective-permute-start.1
  154.0 8.3 collective-permute-start.2
  162.9 9.0 collective-permute-start.3
  215.1 131.6 %all-gather.11.cloned.1.call-start = ((), (), s32[]{:S(2)}) async-start(), calls=%async_computation.9 | async-start | bytes 7208960 | tf_op jit(solution)/shard_map/all_gather | solution.py:186
  215.7 190.0 %all-gather.13.cloned.1.call-start = ((), (), s32[]{:S(2)}) async-start(), calls=%async_computation.10 | async-start | bytes 3604480 | tf_op jit(solution)/shard_map/all_gather | solution.py:187
  216.3 218.2 %all-reduce.34.cloned.1.call-start = ((), (), s32[]{:S(2)}) async-start(), calls=%async_computation.19 | async-start | bytes 4194304 | tf_op jit(solution)/shard_map/psum | solution.py:270
  239.0 113.7 %copy-start.122 = (f32[256]{0:T(256)}, f32[256]{0:T(256)S(1)}, u32[]{:S(2)}) copy-start(f32[256]{0:T(256)S(1)} %get-tuple-element.1115) | copy-start | bytes 3076
  239.0 199.4 %copy-start = (f32[256,1024]{1,0:T(8,128)}, f32[256,1024]{1,0:T(8,128)S(1)}, u32[]{:S(2)}) copy-start(f32[256,1024]{1,0:T(8,128)S(1)} %get-tuple-element.1116) | copy-start | bytes 3145732
  239.1 199.4 %copy-start.96 = (f32[256]{0:T(256)}, f32[256]{0:T(256)S(1)}, u32[]{:S(2)}) copy-start(f32[256]{0:T(256)S(1)} %add_rsqrt_fusion.3) | copy-start | bytes 3076
  414.9 218.8 %reduce-scatter.13.cloned.1.call-start = ((), (), s32[]{:S(2)}) async-start(), calls=%async_computation.13 | async-start | bytes 2621440 | tf_op jit(solution)/shard_map/reduce_scatter | solution.py:345
  447.6 186.1 %reduce-scatter.17.cloned.1.call-start = ((), (), s32[]{:S(2)}) async-start(), calls=%async_computation.15 | async-start | bytes 7208960 | tf_op jit(solution)/shard_map/reduce_scatter | solution.py:348
  472.3 23.8 %copy-start.64 = (f32[4,128,128]{2,1,0:T(8,128)S(1)}, f32[4,128,128]{2,1,0:T(8,128)}, u32[]{:S(2)}) copy-start(f32[4,128,128]{2,1,0:T(8,128)} %copy.641) | copy-start | bytes 786436
  472.3 26.2 %copy-start.73 = (bf16[256,1024]{1,0:T(8,128)(2,1)S(1)}, bf16[256,1024]{1,0:T(8,128)(2,1)}, u32[]{:S(2)}) copy-start(bf16[256,1024]{1,0:T(8,128)(2,1)} %param.33) | copy-start | bytes 1572868
  472.3 26.2 %copy-start.76 = (bf16[256,1408]{1,0:T(8,128)(2,1)S(1)}, bf16[256,1408]{1,0:T(8,128)(2,1)}, u32[]{:S(2)}) copy-start(bf16[256,1408]{1,0:T(8,128)(2,1)} %copy-done.75) | copy-start | bytes 2162692
  473.8 10.4 collective-permute-start.4
  485.5 10.6 collective-permute-start.5
  497.2 10.0 collective-permute-start.6
  502.0 225.1 %reduce-scatter.11.cloned.1.call-start = ((), (), s32[]{:S(2)}) async-start(), calls=%async_computation.12 | async-start | bytes 7864320 | tf_op jit(solution)/shard_map/reduce_scatter | solution.py:341
  513.9 51.5 %copy-start.105 = (f32[4,64]{1,0:T(4,128)S(1)}, f32[4,64]{1,0:T(4,128)}, u32[]{:S(2)}) copy-start(f32[4,64]{1,0:T(4,128)} %slice_bitcast_fusion.4) | copy-start | bytes 3076
  604.7 6.5 collective-permute-start.7
  614.9 309.9 %reduce-scatter.15.cloned.1.call-start = ((), (), s32[]{:S(2)}) async-start(), calls=%async_computation.14 | async-start | bytes 14417920 | tf_op jit(solution)/shard_map/reduce_scatter | solution.py:347
  624.3 326.3 %reduce-scatter.19.cloned.1.call-start = ((), (), s32[]{:S(2)}) async-start(), calls=%async_computation.16 | async-start | bytes 655360
  627.6 343.0 %reduce-scatter.21.cloned.1.call-start = ((), (), s32[]{:S(2)}) async-start(), calls=%async_computation.17 | async-start | bytes 81920
  629.1 362.2 %all-reduce.30.cloned.1.call-start = ((), (), s32[]{:S(2)}) async-start(), calls=%async_computation.11 | async-start | bytes 2097152 | tf_op jit(solution)/shard_map/psum | solution.py:334
  633.6 505.7 %all-reduce.32.cloned.1.call-start = ((), (), s32[]{:S(2)}) async-start(), calls=%async_computation.18 | async-start | bytes 12845056 | tf_op jit(solution)/shard_map/psum | solution.py:351
  931.2 61.9 %copy-start.116 = (f32[1024]{0:T(1024)S(1)}, f32[1024]{0:T(1024)}, u32[]{:S(2)}) copy-start(f32[1024]{0:T(1024)} %get-tuple-element.998) | copy-start | bytes 12292
  931.2 103.7 %copy-start.21 = (f32[256,1024]{1,0:T(8,128)S(1)}, f32[256,1024]{1,0:T(8,128)}, u32[]{:S(2)}) copy-start(f32[256,1024]{1,0:T(8,128)} %copy-done.20) | copy-start | bytes 3145732
  991.3 43.6 %copy-start.65 = (f32[256,1024]{1,0:T(8,128)S(1)}, f32[256,1024]{1,0:T(8,128)}, u32[]{:S(2)}) copy-start(f32[256,1024]{1,0:T(8,128)} %all-reduce.30.cloned.1.call-done) | copy-start | bytes 3145732
  (120 other events, 355.0 us)
Sparse Core Ops, SparseCore 0:
  9.7 72.0 all-gather.6
  83.3 29.4 all-gather.8
  215.2 22.0 all-reduce.27
  238.8 107.8 all-gather.10
  348.3 57.4 all-gather.12
  415.0 19.4 all-reduce.33
  447.7 45.0 reduce-scatter.12
  502.1 105.3 reduce-scatter.16
  615.1 111.9 reduce-scatter.10
  729.4 195.4 reduce-scatter.14
  927.8 22.6 reduce-scatter.18
  953.3 17.2 reduce-scatter.20
  973.5 17.7 all-reduce.29
  995.5 143.7 all-reduce.31
where the time goes:
time: 1160 us; the launch traced here: 1150 us
  waiting for transfers between devices  684 us (59%)
  matrix products  210 us (18%)
  blocking collectives  103 us (9%)
  local copies, waits for them, and re-layouts  84.7 us (7%)
  other arithmetic  28.9 us (2%)
  starting transfers between devices  24 us (2%)
  between operations  19.1 us (2%)
    reduce_scatter x1, waiting for transfers between devices, local(): lax.psum_scatter(gate_up_grad, 'fsdp', scatter_dimension=1, tiled=True)  198 us
    dot_general x123, matrix products, product(): return jnp.einsum(form, left, right, precision=PRECISE)  163 us
    all_gather x1, waiting for transfers between devices, local(): lax.all_gather(gate_up_weight, 'fsdp', axis=1, tiled=True)  108 us
    psum x1, waiting for transfers between devices, local(): lax.psum((shares[0], shares[1], shares[2], shares[3], shares[4], shares[5...  103 us
    reduce_scatter x1, waiting for transfers between devices, local(): lax.psum_scatter(qkv_grad, 'fsdp', scatter_dimension=1, tiled=True)  93.4 us
    all_gather x1, waiting for transfers between devices, local(): lax.all_gather(down_weight, 'fsdp', axis=1, tiled=True)  53 us
    unnamed x16, waiting for transfers between devices  40.8 us
    ppermute x8, waiting for transfers between devices, passed_along(): lax.ppermute(value, axis, [(source, source + steps) for source in range(l...  34.1 us
  transfers between devices with their start and end apart: 22, of which 18 were waited for; matrix products, arithmetic and copies ran while one was open for 25% of the time, Pallas kernels for 0%

commit v1 on v0

--- a/solution.py
+++ b/solution.py
@@ -9,6 +9,37 @@
 CONV = 4
 PRECISE = lax.Precision.HIGHEST
 NORM_EPS = 1e-06
+
+
+def proceed_roads(chunk, which_axis):
+    moved = jax.lax.axis_size(which_axis)
+    ready = jax.lax.axis_index(which_axis)
+    u1, w_next, row_out = (moved, ready, chunk.shape[1])
+    queue = []
+    k = 0
+    while k < u1:
+        queue.append((k, (k + 1) % u1))
+        k = k + 1
+    all_blocks = []
+    k = 0
+    while k < u1:
+        all_blocks.append((k, (k - 1) % u1))
+        k += 1
+    v_now = jnp.zeros((*chunk.shape[:1], u1 * row_out, *chunk.shape[2:]), chunk.dtype)
+    v_now = lax.dynamic_update_slice_in_dim(v_now, chunk, w_next * row_out, axis=1)
+    n_now = aux = chunk
+    arr_now = u1 // 2
+    nth = 1
+    while nth < arr_now + 1:
+        n_now = jax.lax.ppermute(n_now, which_axis, queue)
+        v_now = lax.dynamic_update_slice_in_dim(v_now, n_now, (w_next - nth) % u1 * row_out, axis=1)
+        if nth < u1 - arr_now:
+            aux = jax.lax.ppermute(aux, which_axis, all_blocks)
+            v_now = lax.dynamic_update_slice_in_dim(
+                v_now, aux, (w_next + nth) % u1 * row_out, axis=1
+            )
+        nth += 1
+    return v_now
 
 
 def passed_along(value, axis, steps):
@@ -183,7 +214,7 @@
         lax.all_gather(head_gain, "fsdp", axis=0, tiled=True),
         lax.all_gather(out_weight, "fsdp", axis=1, tiled=True),
         lax.all_gather(mlp_gain, "fsdp", axis=0, tiled=True),
-        lax.all_gather(gate_up_weight, "fsdp", axis=1, tiled=True),
+        proceed_roads(gate_up_weight, which_axis="fsdp"),
         lax.all_gather(down_weight, "fsdp", axis=1, tiled=True),
     )
     (

time: 1160 us -> 1140 us (0.983)
  waiting for transfers between devices: 684 us -> 546 us
  blocking collectives: 103 us -> 174 us
  starting transfers between devices: 24 us -> 49.5 us
  local copies, waits for them, and re-layouts: 84.7 us -> 98.7 us
    all_gather x1 -> x0, waiting for transfers between devices: 108 us -> none  [local(): lax.all_gather(gate_up_weight, 'fsdp', axis=1, tiled=True)]
    all_gather x1, blocking collectives: 9.58 us -> 83.4 us  [local(): lax.all_gather(mlp_gain, 'fsdp', axis=0, tiled=True)]
    all_gather x1, waiting for transfers between devices: 53 us -> 0.01 us  [local(): lax.all_gather(down_weight, 'fsdp', axis=1, tiled=True)]
    ppermute x0 -> x3, waiting for transfers between devices: none -> 33 us  [the longest x2 33 us: proceed_roads(): n_now = jax.lax.ppermute(n_now, which_axis, queue)]
    ppermute x0 -> x3, starting transfers between devices: none -> 25.4 us  [the longest x2 21.6 us: proceed_roads(): n_now = jax.lax.ppermute(n_now, which_axis, queue)]
    unnamed x311 -> x309, local copies, waits for them, and re-layouts: 29.3 us -> 32.3 us
    unnamed x16 -> x15, waiting for transfers between devices: 40.8 us -> 40.4 us
  transfers between devices with their start and end apart: 22 -> 24, of which waited for: 18 -> 16; matrix products, arithmetic and copies ran while one was open for 25% -> 26% of each run, Pallas kernels for 0% -> 0%
where the time goes in v1:
time: 1140 us; the launch traced here: 1130 us
  waiting for transfers between devices  546 us (48%)
  matrix products  216 us (19%)
  blocking collectives  174 us (15%)
  local copies, waits for them, and re-layouts  98.7 us (9%)
  starting transfers between devices  49.5 us (4%)
  other arithmetic  28.4 us (2%)
  between operations  19 us (2%)
    reduce_scatter x1, waiting for transfers between devices, local(): lax.psum_scatter(gate_up_grad, 'fsdp', scatter_dimension=1, tiled=True)  198 us
    dot_general x123, matrix products, product(): return jnp.einsum(form, left, right, precision=PRECISE)  166 us
    psum x1, waiting for transfers between devices, local(): lax.psum((shares[0], shares[1], shares[2], shares[3], shares[4], shares[5...  103 us
    reduce_scatter x1, waiting for transfers between devices, local(): lax.psum_scatter(qkv_grad, 'fsdp', scatter_dimension=1, tiled=True)  93.2 us
    all_gather x1, blocking collectives, local(): lax.all_gather(mlp_gain, 'fsdp', axis=0, tiled=True)  83.4 us
    unnamed x15, waiting for transfers between devices  40.4 us
    ppermute x8, waiting for transfers between devices, passed_along(): lax.ppermute(value, axis, [(source, source + steps) for source in range(l...  34.2 us
    ppermute x2, waiting for transfers between devices, proceed_roads(): n_now = jax.lax.ppermute(n_now, which_axis, queue)  33 us
  transfers between devices with their start and end apart: 24, of which 16 were waited for; matrix products, arithmetic and copies ran while one was open for 26% of the time, Pallas kernels for 0%

profile of v1, /device:TPU:0, one launch (start us, length us, event | category | flops | bytes accessed | tf_op | source)
XLA Modules:
  0.0 1133.3 jit_solution(12386601565736750533)
XLA Ops:
  11.2 19.0 %all_gather.27 = bf16[3,4,4,128]{2,1,0,3:T(4,128)(2,1)S(1)} all-gather(bf16[3,4,4,32]{2,1,0,3:T(4,128)(2,1)S(1)} %copy.589), channel_id=1, replica_groups=mesh['fsdp'=4,'ctx'=4,'tp'=2] {'fsdp'}, dimensions={3}, use_global_device_ids=true | all-gather | bytes 15360 | tf_op jit(solution)/shard_map/all_gather | solution.py:213
  30.5 10.6 all-gather
  44.4 12.1 %all_gather.25 = bf16[1024,4]{0,1:T(4,128)(2,1)S(1)} all-gather(bf16[256,4]{0,1:T(4,128)(2,1)S(1)} %copy-done.132), channel_id=1, replica_groups=mesh['fsdp'=4,'ctx'=4,'tp'=2] {'fsdp'}, dimensions={0}, use_global_device_ids=true | all-gather | bytes 10240 | tf_op jit(solution)/shard_map/all_gather | solution.py:212
  58.1 10.0 all-reduce.14
  69.2 8.9 all-gather.6.cloned.1.call-done
  78.1 2.9 convolution_convert_fusion
  81.1 3.4 collective-permute-start
  86.2 2.9 fusion.96
  89.1 2.9 reshape.310
  118.9 3.1 convolution_bitcast_fusion.12
  124.5 13.7 %while.85 = (s32[]{:T(128)}, f32[4,128,128]{1,2,0:T(8,128)S(1)}, f32[4,128,128]{1,2,0:T(8,128)}, f32[4,4,128,128]{2,3,1,0:T(8,128)S(1)}, f32[4,4,128,128]{2,3,1,0:T(8,128)}, /*index=5*/s32[]{:T(128)}, s32[]{:T(128)}) while((s32[]{:T(128)}, f32[4,128,128]{1,2,0:T(8,128)S(1)}, f32[4,128,128]{1,2,0:T(8,128)}, ...), condition=%wide.region_7.8_spmd.clone, body=%wide.region_6.7_spmd.clone.sunk | while | flops 201457664 | bytes 2885218 | solution.py:271
  140.2 4.2 collective-permute-start.1
  145.9 3.1 collective-permute-done.1
  149.7 4.4 collective-permute-start.2
  155.0 2.9 collective-permute-done.2
  158.6 6.0 collective-permute-start.3
  169.7 33.4 %while.82 = (s32[]{:T(128)}, f32[4,128,128]{1,2,0:T(8,128)}, f32[4,4,64,128]{3,2,1,0:T(8,128)}, f32[4,4,128,128]{2,3,1,0:T(8,128)S(1)}, f32[4,1,64,1]{2,3,1,0:T(...) while((s32[]{:T(128)}, f32[4,128,128]{1,2,0:T(8,128)}, ...), condition=%wide.region_10.11_spmd, body=%wide.region_9.10_spmd.sunk | while | flops 226689024 | bytes 3937437 | solution.py:173
  211.7 3.8 collective-permute-start.5
  215.5 33.0 %collective-permute-done.4 = bf16[2,256,1408]{2,1,0:T(8,128)(2,1)} collective-permute-done((bf16[2,256,1408]{2,1,0:T(8,128)(2,1)}, bf16[2,256,1408]{2,1,0:T(8,128)(2,1)}, u32[]{:S(2)}, u32[]{:S(2)}) %collective-permute-start.4) | collective-permute-done | bytes 1441824 | tf_op jit(solution)/shard_map/ppermute | solution.py:34
  248.6 21.5 %collective-permute-start.6 = (bf16[2,256,1408]{2,1,0:T(8,128)(2,1)}, bf16[2,256,1408]{2,1,0:T(8,128)(2,1)}, u32[]{:S(2)}, u32[]{:S(2)}) collective-permute-start(bf16[2,256,1408]{2,1,0:T(8,128)(2,1)} %collective-permute-done.4), channel_id=1, source_target_pairs={{0,8},{8,16},{16,24},{24,0},{1,9},{9,17},{17,25},{25,1},{2,10},{10... | collective-permute-start | bytes 4325384 | tf_op jit(solution)/shard_map/ppermute | solution.py:34
  270.7 83.4 %all-gather.1 = bf16[4,1,256]{2,1,0:T(2,128)(2,1)S(1)} all-gather(bf16[1,1,256]{2,1,0:T(2,128)(2,1)S(1)} %reshape.333), channel_id=1, replica_groups=mesh['fsdp'=4,'ctx'=4,'tp'=2] {'fsdp'}, dimensions={0}, use_global_device_ids=true | all-gather | bytes 2560 | tf_op jit(solution)/shard_map/all_gather | solution.py:216
  355.4 2.9 broadcast_in_dim.188
  369.0 6.3 fusion.207
  375.3 4.3 fusion.133
  379.6 6.1 convolution_bitcast_fusion.13
  394.8 15.7 %all-reduce.34.cloned.1.call-done = (f32[256,1024]{1,0:T(8,128)}, f32[256,1024]{1,0:T(8,128)}) async-done(((f32[256,1024]{1,0:T(8,128)}, f32[256,1024]{1,0:T(8,128)}), (f32[256,1024]{1,0:T(8,128)}, f32[256,1024]{1,0:T(8,128)})) %all-reduce.34.cloned.1.call-update) | async-done | bytes 2097168 | tf_op jit(solution)/shard_map/psum | solution.py:301
  410.4 3.9 multiply_reduce_fusion.4
  424.5 22.0 %while.86 = (s32[]{:T(128)}, f32[4,128,128]{1,2,0:T(8,128)}, f32[4,4,128,128]{3,2,1,0:T(8,128)}, f32[4,1,64,1]{2,3,1,0:T(1,128)S(1)}, f32[4,4,64,128]{3,2,1,0:T(...) while((s32[]{:T(128)}, f32[4,128,128]{1,2,0:T(8,128)}, ...), condition=%wide.region_21.22_spmd.clone, body=%wide.region_20.21_spmd.clone.sunk | while | flops 226787328 | bytes 2756247 | solution.py:173
  451.1 9.1 collective-permute-done.7
  462.8 9.3 collective-permute-done.8
  474.6 3.5 fusion.195
  478.1 5.2 collective-permute-done.9
  490.0 55.3 %while.84 = (s32[]{:T(128)}, f32[4,128,128]{1,2,0:T(8,128)S(1)}, f32[4,4,64,128]{3,2,0,1:T(8,128)}, f32[4,4,64,128]{3,2,0,1:T(8,128)}, f32[4,4,64,64]{2,3,1,0:T(...) while((s32[]{:T(128)}, f32[4,128,128]{1,2,0:T(8,128)S(1)}, ...), condition=%wide.region_23.24_spmd, body=%wide.region_22.23_spmd.sunk | while | flops 453312512 | bytes 9840613 | solution.py:173
  585.4 4.3 collective-permute-done.10
  589.7 3.9 convolution_bitcast_fusion.10
  594.8 8.1 convolution_bitcast_fusion.9
  608.2 4.2 fusion.102
  612.5 93.2 %reduce-scatter.11.cloned.1.call-done = f32[3,256,512]{1,2,0:T(8,128)} async-done(((f32[3,1024,512]{1,2,0:T(8,128)}), f32[3,256,512]{1,2,0:T(8,128)}) %reduce-scatter.11.cloned.1.call-update) | async-done | bytes 1572880 | tf_op jit(solution)/shard_map/reduce_scatter | solution.py:372
  705.7 198.0 %reduce-scatter.15.cloned.1.call-done = f32[2,256,1408]{1,2,0:T(8,128)} async-done(((f32[2,1024,1408]{1,2,0:T(8,128)}), f32[2,256,1408]{1,2,0:T(8,128)}) %reduce-scatter.15.cloned.1.call-update) | async-done | bytes 2883600 | tf_op jit(solution)/shard_map/reduce_scatter | solution.py:378
  905.9 4.0 stack.42
  910.1 19.1 %reduce-scatter.19.cloned.1.call-done = f32[256,4]{1,0:T(8,128)} async-done(((f32[1024,4]{1,0:T(8,128)}), f32[256,4]{1,0:T(8,128)}) %reduce-scatter.19.cloned.1.call-update) | async-done | bytes 4112
  930.2 19.2 %reduce-scatter.21.cloned.1.call-done = f32[32,48]{1,0:T(8,128)} async-done(((f32[128,48]{1,0:T(8,128)}), f32[32,48]{1,0:T(8,128)}) %reduce-scatter.21.cloned.1.call-update) | async-done | bytes 6160
  950.3 19.6 %all-reduce.30.cloned.1.call-done = f32[256,1024]{1,0:T(8,128)} async-done(((f32[256,1024]{1,0:T(8,128)}), f32[256,1024]{1,0:T(8,128)}) %all-reduce.30.cloned.1.call-update) | async-done | bytes 1048592 | tf_op jit(solution)/shard_map/psum | solution.py:365
  971.7 19.0 %all-reduce.21 = (f32[1024]{0:T(1024)S(1)}, f32[128]{0:T(128)S(1)}, f32[1024]{0:T(1024)S(1)}, f32[4,6]{1,0:T(4,128)S(1)}) all-reduce(f32[1024]{0:T(1024)S(1)} %get-tuple-element.993, f32[128]{0:T(128)S(1)} %multiply_reduce_fusion.10, f32[1024]{0:T(1024)S(1)} %copy-done.117, ...), channel_id=2, replica_groups=mesh['fsdp'=4,'ctx'=4,'tp'=2] {'fsdp'}, use_global_device_ids=true, to_apply=%region_31.32.clone | all-reduce | flops 2200 | bytes 17600
  993.8 17.8 %all-reduce.19 = (f32[256]{0:T(256)}, f32[256,4]{0,1:T(4,128)}, f32[3,4,4,32]{3,2,1,0:T(4,128)}, f32[32]{0:T(128)}, f32[256]{0:T(256)}, /*index=5*/f32[1,6]{1,0:T(1,128)S(1)}) all-reduce(f32[256]{0:T(256)S(1)} %dynamic-slice.2, f32[256,4]{0,1:T(4,128)S(1)} %copy.747, ...), channel_id=1, replica_groups=mesh['fsdp'=4,'ctx'=4,'tp'=2] {'ctx'}, use_global_device_ids=true, to_apply=%region_32.33 | all-reduce | flops 3110 | bytes 24880 | tf_op jit(solution)/shard_map/psum | solution.py:382
  1014.7 103.3 %all-reduce.32.cloned.1.call-done = (f32[3,256,512]{1,2,0:T(8,128)}, f32[512,256]{1,0:T(8,128)}, f32[2,256,1408]{1,2,0:T(8,128)}, f32[1408,256]{1,0:T(8,128)}) async-done(((f32[3,256,512]{1,2,0:T(8,128)}, f32[512,256]{1,0:T(8,128)}, f32[2,256,1408]{1,2,0:T(8,128)}, f32[1408,256]{1,0:T(8,128)}), (f32[3,256,512]{1,2,0:T(8,128)}, f32[512,256]{1,0:T(8,128)}, f32[2,256,1408]{1,2,0:T(8,128)}, ...) | async-done | bytes 6422544 | tf_op jit(solution)/shard_map/psum | solution.py:382
  1118.0 3.0 copy.686
  1121.1 3.5 copy.687
  (652 shorter events, 291.7 us)
Async XLA Ops:
  7.2 49.4 %copy-start.134 = (u32[32]{0:T(128)S(1)}, u32[32]{0:T(128)}, u32[]{:S(2)}) copy-start(u32[32]{0:T(128)} %constant.265) | copy-start | bytes 388
  7.2 23.3 %copy-start.139 = (bf16[256]{0:T(256)(128)(2,1)S(1)}, bf16[256]{0:T(256)(128)(2,1)}, u32[]{:S(2)}) copy-start(bf16[256]{0:T(256)(128)(2,1)} %param.24) | copy-start | bytes 1540
  7.2 34.0 %copy-start.11 = (bf16[256,1024]{1,0:T(8,128)(2,1)S(1)}, bf16[256,1024]{1,0:T(8,128)(2,1)}, u32[]{:S(2)}) copy-start(bf16[256,1024]{1,0:T(8,128)(2,1)} %param.22) | copy-start | bytes 1572868
  7.2 37.2 %copy-start.132 = (bf16[256,4]{0,1:T(4,128)(2,1)S(1)}, bf16[256,4]{0,1:T(4,128)(2,1)}, u32[]{:S(2)}) copy-start(bf16[256,4]{0,1:T(4,128)(2,1)} %param.26) | copy-start | bytes 6148
  7.2 50.6 %copy-start.140 = (bf16[32]{0:T(256)(128)(2,1)S(1)}, bf16[32]{0:T(256)(128)(2,1)}, u32[]{:S(2)}) copy-start(bf16[32]{0:T(256)(128)(2,1)} %param.28) | copy-start | bytes 196
  7.2 70.9 %all-gather.6.cloned.1.call-start = ((), (), s32[]{:S(2)}) async-start(), calls=%async_computation.6 | async-start | bytes 3932160 | tf_op jit(solution)/shard_map/all_gather | solution.py:211
  8.0 200.3 %all-gather.8.cloned.1.call-start = ((), (), s32[]{:S(2)}) async-start(), calls=%async_computation.7 | async-start | bytes 1310720 | tf_op jit(solution)/shard_map/all_gather | solution.py:215
  8.7 358.5 %all-reduce.28.cloned.1.call-start = ((), (), s32[]{:S(2)}) async-start(), calls=%async_computation.8 | async-start | bytes 2097152 | tf_op jit(solution)/shard_map/psum | solution.py:289
  8.8 60.4 %copy-start.82 = (f32[128,128]{0,1:T(8,128)}, f32[128,128]{0,1:T(8,128)S(1)}, u32[]{:S(2)}) copy-start(f32[128,128]{0,1:T(8,128)S(1)} %fusion.204) | copy-start | bytes 196612
  10.3 75.9 %copy-start.109 = (f32[256,1]{0,1:T(1,128)}, f32[256,1]{0,1:T(1,128)S(1)}, u32[]{:S(2)}) copy-start(f32[256,1]{0,1:T(1,128)S(1)} %get-tuple-element.1145) | copy-start | bytes 3076
  10.3 75.9 %copy-start.111 = (f32[256,1]{0,1:T(1,128)}, f32[256,1]{0,1:T(1,128)S(1)}, u32[]{:S(2)}) copy-start(f32[256,1]{0,1:T(1,128)S(1)} %get-tuple-element.1146) | copy-start | bytes 3076
  10.3 75.9 %copy-start.113 = (f32[256,1]{0,1:T(1,128)}, f32[256,1]{0,1:T(1,128)S(1)}, u32[]{:S(2)}) copy-start(f32[256,1]{0,1:T(1,128)S(1)} %get-tuple-element.1147) | copy-start | bytes 3076
  10.3 75.9 %copy-start.115 = (f32[256,1]{0,1:T(1,128)}, f32[256,1]{0,1:T(1,128)S(1)}, u32[]{:S(2)}) copy-start(f32[256,1]{0,1:T(1,128)S(1)} %get-tuple-element.1148) | copy-start | bytes 3076
  41.9 39.1 %copy-start.107 = (f32[256]{0:T(256)}, f32[256]{0:T(256)S(1)}, u32[]{:S(2)}) copy-start(f32[256]{0:T(256)S(1)} %add_rsqrt_fusion.4) | copy-start | bytes 3076
  56.5 24.5 %copy-start.101 = (bf16[1024,4]{0,1:T(4,128)(2,1)}, bf16[1024,4]{0,1:T(4,128)(2,1)S(1)}, u32[]{:S(2)}) copy-start(bf16[1024,4]{0,1:T(4,128)(2,1)S(1)} %all_gather.25) | copy-start | bytes 24580
  68.7 17.4 %copy-start.85 = (f32[3,512]{1,0:T(4,128)}, f32[3,512]{1,0:T(4,128)S(1)}, u32[]{:S(2)}) copy-start(f32[3,512]{1,0:T(4,128)S(1)} %get-tuple-element.1158) | copy-start | bytes 18436
  81.1 4.8 collective-permute-start
  140.2 8.8 collective-permute-start.1
  149.7 8.3 collective-permute-start.2
  158.6 9.2 collective-permute-start.3
  208.3 61.9 %copy-start.137 = (s32[4,1]{0,1:T(1,128)S(1)}, s32[4,1]{0,1:T(1,128)}, u32[]{:S(2)}) copy-start(s32[4,1]{0,1:T(1,128)} %copy-done.136) | copy-start | bytes 52
  208.3 62.4 %copy-start.141 = (bf16[256]{0:T(256)(128)(2,1)S(1)}, bf16[256]{0:T(256)(128)(2,1)}, u32[]{:S(2)}) copy-start(bf16[256]{0:T(256)(128)(2,1)} %param.30) | copy-start | bytes 1540
  211.0 164.2 %all-gather.10.cloned.1.call-start = ((), (), s32[]{:S(2)}) async-start(), calls=%async_computation.9 | async-start | bytes 3604480 | tf_op jit(solution)/shard_map/all_gather | solution.py:218
  211.6 198.8 %all-reduce.34.cloned.1.call-start = ((), (), s32[]{:S(2)}) async-start(), calls=%async_computation.18 | async-start | bytes 4194304 | tf_op jit(solution)/shard_map/psum | solution.py:301
  211.7 36.9 %collective-permute-start.4 = (bf16[2,256,1408]{2,1,0:T(8,128)(2,1)}, bf16[2,256,1408]{2,1,0:T(8,128)(2,1)}, u32[]{:S(2)}, u32[]{:S(2)}) collective-permute-start(bf16[2,256,1408]{2,1,0:T(8,128)(2,1)} %param.31), channel_id=1, source_target_pairs={{0,8},{8,16},{16,24},{24,0},{1,9},{9,17},{17,25},{25,1},{2,10},{10... | collective-permute-start | bytes 4325384 | tf_op jit(solution)/shard_map/ppermute | solution.py:34
  211.7 150.3 %collective-permute-start.5 = (bf16[2,256,1408]{2,1,0:T(8,128)(2,1)}, bf16[2,256,1408]{2,1,0:T(8,128)(2,1)}, u32[]{:S(2)}, u32[]{:S(2)}) collective-permute-start(bf16[2,256,1408]{2,1,0:T(8,128)(2,1)} %param.31), channel_id=1, source_target_pairs={{0,24},{8,0},{16,8},{24,16},{1,25},{9,1},{17,9},{25,17},{2,26},{10... | collective-permute-start | bytes 4325384 | tf_op jit(solution)/shard_map/ppermute | solution.py:37
  248.6 116.0 %collective-permute-start.6 = (bf16[2,256,1408]{2,1,0:T(8,128)(2,1)}, bf16[2,256,1408]{2,1,0:T(8,128)(2,1)}, u32[]{:S(2)}, u32[]{:S(2)}) collective-permute-start(bf16[2,256,1408]{2,1,0:T(8,128)(2,1)} %collective-permute-done.4), channel_id=1, source_target_pairs={{0,8},{8,16},{16,24},{24,0},{1,9},{9,17},{17,25},{25,1},{2,10},{10... | collective-permute-start | bytes 4325384 | tf_op jit(solution)/shard_map/ppermute | solution.py:34
  368.9 45.4 %copy-start = (f32[256,1024]{1,0:T(8,128)}, f32[256,1024]{1,0:T(8,128)S(1)}, u32[]{:S(2)}) copy-start(f32[256,1024]{1,0:T(8,128)S(1)} %get-tuple-element.1116) | copy-start | bytes 3145732
  369.0 45.4 %copy-start.97 = (f32[256]{0:T(256)}, f32[256]{0:T(256)S(1)}, u32[]{:S(2)}) copy-start(f32[256]{0:T(256)S(1)} %add_rsqrt_fusion.3) | copy-start | bytes 3076
  387.7 224.7 %reduce-scatter.13.cloned.1.call-start = ((), (), s32[]{:S(2)}) async-start(), calls=%async_computation.12 | async-start | bytes 2621440 | tf_op jit(solution)/shard_map/reduce_scatter | solution.py:376
  423.6 188.9 %reduce-scatter.17.cloned.1.call-start = ((), (), s32[]{:S(2)}) async-start(), calls=%async_computation.14 | async-start | bytes 7208960 | tf_op jit(solution)/shard_map/reduce_scatter | solution.py:379
  448.3 23.8 %copy-start.64 = (f32[4,128,128]{2,1,0:T(8,128)S(1)}, f32[4,128,128]{2,1,0:T(8,128)}, u32[]{:S(2)}) copy-start(f32[4,128,128]{2,1,0:T(8,128)} %copy.641) | copy-start | bytes 786436
  448.3 26.2 %copy-start.73 = (bf16[256,1024]{1,0:T(8,128)(2,1)S(1)}, bf16[256,1024]{1,0:T(8,128)(2,1)}, u32[]{:S(2)}) copy-start(bf16[256,1024]{1,0:T(8,128)(2,1)} %param.33) | copy-start | bytes 1572868
  448.3 26.2 %copy-start.75 = (bf16[256,1408]{1,0:T(8,128)(2,1)S(1)}, bf16[256,1408]{1,0:T(8,128)(2,1)}, u32[]{:S(2)}) copy-start(bf16[256,1408]{1,0:T(8,128)(2,1)} %copy-done.74) | copy-start | bytes 2162692
  449.8 10.4 collective-permute-start.7
  461.5 10.6 collective-permute-start.8
  473.2 10.0 collective-permute-start.9
  478.0 227.6 %reduce-scatter.11.cloned.1.call-start = ((), (), s32[]{:S(2)}) async-start(), calls=%async_computation.11 | async-start | bytes 7864320 | tf_op jit(solution)/shard_map/reduce_scatter | solution.py:372
  490.0 55.3 %copy-start.104 = (f32[4,64]{1,0:T(4,128)S(1)}, f32[4,64]{1,0:T(4,128)}, u32[]{:S(2)}) copy-start(f32[4,64]{1,0:T(4,128)} %get-tuple-element.1119) | copy-start | bytes 3076
  583.2 6.5 collective-permute-start.10
  593.6 310.0 %reduce-scatter.15.cloned.1.call-start = ((), (), s32[]{:S(2)}) async-start(), calls=%async_computation.13 | async-start | bytes 14417920 | tf_op jit(solution)/shard_map/reduce_scatter | solution.py:378
  603.0 326.2 %reduce-scatter.19.cloned.1.call-start = ((), (), s32[]{:S(2)}) async-start(), calls=%async_computation.15 | async-start | bytes 655360
  606.4 342.9 %reduce-scatter.21.cloned.1.call-start = ((), (), s32[]{:S(2)}) async-start(), calls=%async_computation.16 | async-start | bytes 81920
  607.9 362.0 %all-reduce.30.cloned.1.call-start = ((), (), s32[]{:S(2)}) async-start(), calls=%async_computation.10 | async-start | bytes 2097152 | tf_op jit(solution)/shard_map/psum | solution.py:365
  612.4 505.7 %all-reduce.32.cloned.1.call-start = ((), (), s32[]{:S(2)}) async-start(), calls=%async_computation.17 | async-start | bytes 12845056 | tf_op jit(solution)/shard_map/psum | solution.py:382
  909.8 61.8 %copy-start.117 = (f32[1024]{0:T(1024)S(1)}, f32[1024]{0:T(1024)}, u32[]{:S(2)}) copy-start(f32[1024]{0:T(1024)} %get-tuple-element.998) | copy-start | bytes 12292
  909.8 103.6 %copy-start.21 = (f32[256,1024]{1,0:T(8,128)S(1)}, f32[256,1024]{1,0:T(8,128)}, u32[]{:S(2)}) copy-start(f32[256,1024]{1,0:T(8,128)} %copy-done.20) | copy-start | bytes 3145732
  969.9 43.6 %copy-start.65 = (f32[256,1024]{1,0:T(8,128)S(1)}, f32[256,1024]{1,0:T(8,128)}, u32[]{:S(2)}) copy-start(f32[256,1024]{1,0:T(8,128)} %all-reduce.30.cloned.1.call-done) | copy-start | bytes 3145732
  (121 other events, 383.6 us)
Sparse Core Ops, SparseCore 0:
  9.6 68.4 all-gather.5
  79.7 29.1 all-gather.7
  211.2 21.5 all-reduce.27
  234.2 116.0 all-gather.9
  387.8 22.5 all-reduce.33
  423.7 45.0 reduce-scatter.12
  478.2 105.3 reduce-scatter.16
  593.7 111.8 reduce-scatter.10
  708.1 195.4 reduce-scatter.14
  906.4 22.6 reduce-scatter.18
  932.1 17.1 reduce-scatter.20
  952.1 17.7 all-reduce.29
  974.2 143.7 all-reduce.31
